TPU v7x, 256 devices: a whole 4x4x8 slice. The times are simulated.
256 devices in a mesh: tm: 64 (over x, z, core), space: 4 (over y).
Axes of the slice: x: 4, y: 4, z: 8, core: 2. Of those that a mesh axis runs over, the one named last changes fastest.
Arguments:
- snapshots: float32 [4096, 16384], P('tm', 'space'), as said below
- space_factor: float32 [16384, 256], P('space'), as said below
Outputs:
- time_factor: float32 [4096, 256], P('tm')
- loadings: float32 [256, 16384], P('tm', 'space')
Inputs may be any that keep to these rules, and one draw needn't show every extreme that they name: `snapshots`: entries are real values. `space_factor`: entries are real values; columns have norms between 0.05 and 1, the previous sweep's singular values.
All inputs are finite; a program needn't handle non-finite values.
Results may differ from a plain program's by a relative error of at most 0.0001.
Values sent between devices are 32-bit elements; how exact they have to be, the bound alone decides.
A program may use at most 64 MiB of HBM per device.

v0:
```python
import math

import jax
import jax.numpy as jnp
from jax import lax
from jax.sharding import PartitionSpec as P

RANK = 256
NS = 2


def inner(left, right):
    return lax.dot_general(
        left,
        right,
        (((0,), (0,)), ((), ())),
        precision=lax.Precision.HIGHEST,
        preferred_element_type=jnp.float32,
    )


def matmul(left, right):
    return jnp.dot(left, right, precision=lax.Precision.HIGHEST, preferred_element_type=jnp.float32)


def on_device(snapshots, space_factor):
    projected = lax.psum(matmul(snapshots, space_factor), "space")
    devices = lax.axis_size("tm")
    scaling = jnp.float32(math.sqrt(devices * snapshots.shape[0]))
    energy = lax.psum(jnp.sum(projected * projected), "tm")
    factor = projected / jnp.sqrt(energy)
    identity_mat = jnp.eye(RANK, dtype=jnp.float32)

    def advance(sweep, current):
        correlation = lax.psum(inner(current, current), "tm")
        return matmul(current, 1.5 * identity_mat - 0.5 * correlation)

    factor = lax.fori_loop(0, NS, advance, factor)
    loadings = lax.psum_scatter(inner(factor, snapshots), "tm", scatter_dimension=0, tiled=True)
    return (factor * scaling, loadings)


def solution(mesh):
    return jax.shard_map(
        on_device,
        mesh=mesh,
        in_specs=(P("tm", "space"), P("space", None)),
        out_specs=(P("tm", None), P("tm", "space")),
        check_vma=False,
    )
```

profile of v0, /device:TPU:1, one launch (start us, length us, event | category | flops | bytes accessed | tf_op | source)
XLA Modules:
  0.0 756.1 jit_solution(8482115746510413596)
XLA Ops:
  7.2 0.0 copy-start
  7.2 0.0 all-reduce.5.cloned.1.call-start
  7.2 1.2 copy-done
  8.4 5.1 fusion.10
  13.5 0.0 all-reduce.5.cloned.1.call-update
  13.5 48.3 %all-reduce.5.cloned.1.call-done = f32[64,256]{1,0:T(8,128)} async-done(((f32[64,256]{1,0:T(8,128)}), f32[64,256]{1,0:T(8,128)}) %all-reduce.5.cloned.1.call-update) | async-done | bytes 65552 | tf_op jit(solution)/shard_map/psum | solution.py:27
  61.7 1.5 multiply_reduce_fusion
  63.2 127.2 %psum.22 = f32[]{:T(128)} all-reduce(f32[]{:T(128)} %multiply_reduce_fusion), channel_id=1, replica_groups=mesh['tm'=64,'space'=4] {'tm'}, use_global_device_ids=true, to_apply=%region_2.0 | all-reduce | flops 1 | bytes 8 | tf_op jit(solution)/shard_map/psum | solution.py:30
  191.1 0.9 broadcast_divide_fusion
  191.9 359.3 %while.11 = (s32[]{:T(128)}, f32[64,256]{1,0:T(8,128)S(1)}, s32[]{:T(128)}) while((s32[]{:T(128)}, f32[64,256]{1,0:T(8,128)S(1)}, s32[]{:T(128)}) %tuple.25), condition=%wide.region_5.0_spmd.clone, body=%wide.region_3.0_spmd.clone.sunk | while | flops 100990976 | bytes 2424917 | solution.py:38
  192.0 0.0 all-reduce.9.cloned.1.call-start
  192.0 1.1 fusion.26
  193.1 0.0 all-reduce.9.cloned.1.call-update
  193.2 176.3 %all-reduce.9.cloned.1.call-done = f32[256,256]{1,0:T(8,128)} async-done(((f32[256,256]{1,0:T(8,128)}), f32[256,256]{1,0:T(8,128)}) %all-reduce.9.cloned.1.call-update) | async-done | bytes 262160 | tf_op jit(solution)/shard_map/while/body/eval_jaxpr/psum | solution.py:35
  369.5 1.3 convolution_bitcast_fusion.2
  370.7 0.0 all-reduce.9.cloned.1.call-start
  370.8 1.1 fusion.26
  371.9 0.0 all-reduce.9.cloned.1.call-update
  372.0 178.0 %all-reduce.9.cloned.1.call-done = f32[256,256]{1,0:T(8,128)} async-done(((f32[256,256]{1,0:T(8,128)}), f32[256,256]{1,0:T(8,128)}) %all-reduce.9.cloned.1.call-update) | async-done | bytes 262160 | tf_op jit(solution)/shard_map/while/body/eval_jaxpr/psum | solution.py:35
  550.0 1.3 convolution_bitcast_fusion.2
  551.2 0.0 all-reduce.7.cloned.1.call-start
  551.3 0.0 copy-start.1
  551.3 5.1 fusion.11
  556.4 0.0 all-reduce.7.cloned.1.call-update
  556.5 0.0 copy-done.1
  556.5 0.6 dynamic-slice
  557.7 0.6 broadcast_multiply_fusion
  558.3 189.6 %all-reduce.7.cloned.1.call-done = f32[256,4096]{1,0:T(8,128)} async-done(((f32[256,4096]{1,0:T(8,128)}), f32[256,4096]{1,0:T(8,128)}) %all-reduce.7.cloned.1.call-update) | async-done | bytes 4194320
  748.0 1.5 constant_dynamic-slice_fusion
  (2 shorter events, 0.0 us)
Async XLA Ops:
  7.2 1.2 copy-start
  7.2 54.6 %all-reduce.5.cloned.1.call-start = ((), (), s32[]{:S(2)}) async-start(), calls=%async_computation | async-start | bytes 131072 | tf_op jit(solution)/shard_map/psum | solution.py:27
  192.0 177.5 %all-reduce.9.cloned.1.call-start = ((), (), s32[]{:S(2)}) async-start(), calls=%async_computation.2 | async-start | bytes 524288 | tf_op jit(solution)/shard_map/while/body/eval_jaxpr/psum | solution.py:35
  370.7 179.2 %all-reduce.9.cloned.1.call-start = ((), (), s32[]{:S(2)}) async-start(), calls=%async_computation.2 | async-start | bytes 524288 | tf_op jit(solution)/shard_map/while/body/eval_jaxpr/psum | solution.py:35
  551.2 196.7 %all-reduce.7.cloned.1.call-start = ((), (), s32[]{:S(2)}) async-start(), calls=%async_computation.1 | async-start | bytes 8388608
  551.3 5.2 copy-start.1
Sparse Core Ops, SparseCore 0:
  13.6 48.0 all-reduce.4
  196.2 173.1 all-reduce.8
  375.0 174.8 all-reduce.8
  556.6 191.3 all-reduce.6
where the time goes:
time: 757 us; the launch traced here: 756 us
  waiting for transfers between devices  592 us (78%)
  blocking collectives  127 us (17%)
  between operations  15.1 us (2%)
  matrix products  15 us (2%)
    psum x2, waiting for transfers between devices, advance(): correlation = lax.psum(inner(current, current), 'tm')  354 us
    unnamed x3, waiting for transfers between devices  190 us
    psum x1, blocking collectives, on_device(): energy = lax.psum(jnp.sum(projected * projected), 'tm')  127 us
    psum x1, waiting for transfers between devices, on_device(): projected = lax.psum(matmul(snapshots, space_factor), 'space')  48.3 us
  transfers between devices with their start and end apart: 4, of which 4 were waited for; matrix products, arithmetic and copies ran while one was open for 0% of the time, Pallas kernels for 0%

commit v1 on v0

v1 whole, which is shorter than its diff:
```python
import math

import jax
import jax.numpy as jnp
from jax import lax
from jax.experimental import pallas as pl
from jax.experimental.pallas import tpu as pltpu
from jax.sharding import PartitionSpec as P

MESH = pl.DeviceIdType.MESH
F32, BF16 = jnp.float32, jnp.bfloat16
RANK = 256
TIME = 4096
NX, NY, NZ = 4, 4, 8
ROWS = 64
COLS = 4096
WIDE = COLS // NX
CHUNK = WIDE // NZ
HALF = RANK // 2
LOADS = 8
EARLY = 3


def split(value):
    high = value.astype(BF16)
    return high, (value - high.astype(F32)).astype(BF16)


def dot(left, right, dims=((1,), (0,))):
    return lax.dot_general(left, right, (dims, ((), ())), preferred_element_type=F32)


def dot3(left, right, dims=((1,), (0,))):
    return dot(left[0], right[0], dims) + (dot(left[0], right[1], dims) + dot(left[1], right[0], dims))


def kernel(
    snap_hbm, space_hbm, time_out, load_out,
    xv, sv, part, pair, from_y, yg, yt, xg, gram, gram_x, gram_z, corr, fth, ftl,
    lp, lp_peer, up, up_in, down, down_in, full, mixed, land,
    ld_x, ld_s, xs, xr, ys, yr, ags, agr, gxs, gxr, gzs, gzr, cs, cr, ps, pr,
    us, ur, ds, dr, fs, fr, ms, mr,
):
    t, y = lax.axis_index("tm"), lax.axis_index("space")
    x, z, c = t // 16, (t // 2) % NZ, t % 2
    other = 1 - c

    def dev(x_, y_, z_, c_):
        return {"tm": x_ * 16 + z_ * 2 + c_, "space": y_}

    def remote(src, dst, send, recv, to):
        return pltpu.make_async_remote_copy(
            src_ref=src, dst_ref=dst, send_sem=send, recv_sem=recv, device_id=to, device_id_type=MESH
        )

    partner = dev(x, y, z, other)
    flip_a = dev(x, y + 1 - 2 * (y % 2), z, c)
    flip_b = dev(x, NY - 1 - y, z, c)

    load_x = pltpu.make_async_copy(snap_hbm, xv, ld_x)
    load_x.start()
    depth = COLS // LOADS
    load_s = [
        pltpu.make_async_copy(space_hbm.at[pl.ds(i * depth, depth)], sv.at[pl.ds(i * depth, depth)], ld_s.at[i])
        for i in range(LOADS)
    ]
    for copy in load_s:
        copy.start()

    barrier = pltpu.get_barrier_semaphore()
    greeted = [flip_a, flip_b, partner]
    greeted += [dev((x + i) % NX, y, z, k) for i in range(1, NX) for k in range(2)]
    greeted += [dev(x, y, (z + i) % NZ, c) for i in range(1, NZ)]
    for to in greeted:
        pl.semaphore_signal(barrier, inc=1, device_id=to, device_id_type=MESH)

    load_x.wait()
    acc = jnp.zeros((ROWS, RANK), F32)
    acc2 = jnp.zeros((2 * ROWS, RANK), F32)
    for i in range(LOADS):
        load_s[i].wait()
        xh, xl = split(xv[:, i * depth:(i + 1) * depth])
        sh, sl = split(sv[i * depth:(i + 1) * depth, :])
        acc2 = acc2 + dot(jnp.concatenate([xh, xl], axis=0), sh)
        acc = acc + dot(xh, sl)
    part[...] = acc2[:ROWS] + (acc2[ROWS:] + acc)
    pl.semaphore_wait(barrier, len(greeted))

    top, low = pl.ds(0, ROWS // 2), pl.ds(ROWS // 2, ROWS // 2)
    first = [
        remote(part.at[top], from_y.at[0], ys.at[0], yr.at[0], flip_a),
        remote(part.at[low], from_y.at[1], ys.at[1], yr.at[1], flip_b),
    ]
    for copy in first:
        copy.start()

    order = [(z + 4) % NZ, (z + 5) % NZ, (z + 3) % NZ, (z + 6) % NZ, (z + 2) % NZ, (z + 7) % NZ, (z + 1) % NZ, z]

    def send_columns(slots):
        for s in slots:
            for i in (2, 1, 3):
                xp = (x + i) % NX
                at = pl.multiple_of(xp * WIDE + order[s] * CHUNK, CHUNK)
                remote(xv.at[:, pl.ds(at, CHUNK)], xg.at[order[s], x], xs, xr.at[s], dev(xp, y, z, c)).start()

    send_columns(range(EARLY))
    for d in range(NZ):
        xg[d, x] = xv[:, pl.ds(pl.multiple_of(x * WIDE + d * CHUNK, CHUNK), CHUNK)]

    first[0].wait_recv()
    pair[:ROWS // 2] = part[:ROWS // 2] + from_y[0]
    second = [remote(pair.at[top], from_y.at[2], ys.at[2], yr.at[2], flip_b)]
    second[0].start()
    first[1].wait_recv()
    pair[ROWS // 2:] = part[ROWS // 2:] + from_y[1]
    second.append(remote(pair.at[low], from_y.at[3], ys.at[3], yr.at[3], flip_a))
    second[1].start()
    second[0].wait_recv()
    second[1].wait_recv()
    mine = jnp.concatenate([pair[:ROWS // 2] + from_y[2], pair[ROWS // 2:] + from_y[3]], axis=0)
    yg[x] = mine

    parts = split(mine)
    share = dot3(parts, parts, ((0,), (0,)))
    energy = jnp.sum(jnp.sum(mine * mine, axis=0, keepdims=True), axis=1, keepdims=True)
    energy = jnp.broadcast_to(energy, (8, 128))
    for b in range(NY):
        for k in range(8):
            gram[b, k, :, :RANK] = share[64 * b + 8 * k:64 * b + 8 * k + 8]
            gram[b, k, :, RANK:] = energy
    me8 = 2 * x + c
    gram_x[me8] = gram[y, me8]
    for i in (2, 1, 3, 0):
        for k in range(2):
            if i == 0 and k == 0:
                continue
            xp, cp = (x + i) % NX, (c + k) % 2
            remote(gram.at[y, 2 * xp + cp], gram_x.at[me8], gxs, gxr, dev(xp, y, z, cp)).start()

    for i in (2, 1, 3):
        remote(yg.at[x], yg.at[x], ags, agr, dev((x + i) % NX, y, z, c)).start()
    send_columns(range(EARLY, NZ))

    remote(gram_x.at[pl.ds(0, 7)], gram_x.at[pl.ds(0, 7)], gxs, gxr, partner).wait_recv()
    total = gram_x[0]
    for k in range(1, 8):
        total = total + gram_x[k]
    gram_z[z] = total
    for i in (4, 3, 5, 2, 6, 1, 7):
        remote(gram_z.at[z], gram_z.at[z], gzs, gzr, dev(x, y, (z + i) % NZ, c)).start()

    remote(yg.at[pl.ds(0, 3)], yg.at[pl.ds(0, 3)], ags, agr, partner).wait_recv()
    for i in range(NX):
        yt[:, i * ROWS:(i + 1) * ROWS] = yg[i].T

    remote(gram_z.at[pl.ds(0, 7)], gram_z.at[pl.ds(0, 7)], gzs, gzr, partner).wait_recv()
    total = gram_z[0]
    for k in range(1, NZ):
        total = total + gram_z[k]
    block = 8 * y + me8
    corr[block] = total[:, :RANK]
    scale = 1.0 / jnp.sqrt(total[0:1, RANK:RANK + 1])
    for i in (2, 1, 3, 0):
        for j in (2, 1, 3, 0):
            for k in range(2):
                if i == 0 and j == 0 and k == 0:
                    continue
                to = dev((x + i) % NX, (y + j) % NY, z, (c + k) % 2)
                remote(corr.at[block], corr.at[block], cs, cr, to).start()

    fth[...], ftl[...] = split(yt[...] * scale)
    swaps = [None] * NZ

    def form(s):
        d = order[s]
        remote(xg.at[d, pl.ds(0, 3)], xg.at[d, pl.ds(0, 3)], xs, xr.at[s], partner).wait_recv()
        cols = split(xg[d].reshape(NX * ROWS, CHUNK))
        value = dot3((fth[...], ftl[...]), cols)
        lp[d, 0] = value[:HALF]
        lp[d, 1] = value[HALF:]
        swaps[s] = remote(lp.at[d, other], lp_peer.at[d], ps.at[s], pr.at[s], partner)
        swaps[s].start()

    def held(s):
        swaps[s].wait_recv()
        return lp[order[s], c] + lp_peer[order[s]]

    above, below = dev(x, y, (z + 1) % NZ, c), dev(x, y, (z + 7) % NZ, c)
    ups = [remote(up.at[s], up_in.at[s], us.at[s], ur.at[s], above) for s in range(4)]
    downs = [remote(down.at[s], down_in.at[s], ds.at[s], dr.at[s], below) for s in range(3)]

    for s in range(4):
        form(s)
    up[0] = held(0)
    ups[0].start()
    down[0] = held(1)
    downs[0].start()
    form(4)
    form(5)
    for s in range(1, 3):
        value = held(2 * s)
        ups[s - 1].wait_recv()
        up[s] = value + up_in[s - 1]
        ups[s].start()
        value = held(2 * s + 1)
        downs[s - 1].wait_recv()
        down[s] = value + down_in[s - 1]
        downs[s].start()
        if s == 1:
            form(6)
            form(7)

    remote(corr.at[pl.ds(0, 31)], corr.at[pl.ds(0, 31)], cs, cr, partner).wait_recv()
    a1 = corr[...].reshape(RANK, RANK) * scale * scale
    a1s = split(a1)
    a2 = dot3(a1s, a1s)
    a4 = dot3(split(a2), split(a2 - 9.0 * a1))
    row = lax.broadcasted_iota(jnp.int32, (RANK, RANK), 0)
    col = lax.broadcasted_iota(jnp.int32, (RANK, RANK), 1)
    poly = jnp.where(row == col, 2.25, 0.0) + (a4 + (27.0 * a2 - 39.0 * a1)) * 0.0625
    polys = split(poly)

    value = held(6)
    ups[2].wait_recv()
    up[3] = value + up_in[2]
    ups[3].start()
    time_out[...] = dot3(split(yg[x] * scale), polys) * math.sqrt(TIME)
    value = held(7)
    downs[2].wait_recv()
    value = value + down_in[2]
    ups[3].wait_recv()
    full[c] = value + up_in[3]
    share_full = remote(full.at[c], full.at[c], fs, fr, partner)
    share_full.start()
    share_full.wait_recv()

    value = dot3(polys, split(full[...].reshape(RANK, CHUNK)))
    value = jnp.where(c == 0, value, pltpu.roll(value, RANK - 4, 0))
    for k in range(NX * NZ):
        mixed[k] = value[8 * k:8 * k + 4]
    spot = NZ * x + z
    land[spot] = mixed[spot]
    for i in (2, 1, 3, 0):
        for j in (4, 3, 5, 2, 6, 1, 7, 0):
            if i == 0 and j == 0:
                continue
            xp, zp = (x + i) % NX, (z + j) % NZ
            remote(mixed.at[NZ * xp + zp], land.at[spot], ms, mr, dev(xp, y, zp, c)).start()
    remote(land.at[pl.ds(0, 31)], land.at[pl.ds(0, 31)], ms, mr, partner).wait_recv()
    for k in range(NX * NZ):
        load_out[:, k * CHUNK:(k + 1) * CHUNK] = land[k]

    for copy in first + second + swaps + ups + downs + [share_full]:
        copy.wait_send()
    remote(xg.at[pl.ds(0, 6)], xg.at[pl.ds(0, 6)], xs, xr.at[0], partner).wait_send()
    remote(yg.at[pl.ds(0, 3)], yg.at[pl.ds(0, 3)], ags, agr, partner).wait_send()
    remote(gram_x.at[pl.ds(0, 7)], gram_x.at[pl.ds(0, 7)], gxs, gxr, partner).wait_send()
    remote(gram_z.at[pl.ds(0, 7)], gram_z.at[pl.ds(0, 7)], gzs, gzr, partner).wait_send()
    remote(corr.at[pl.ds(0, 31)], corr.at[pl.ds(0, 31)], cs, cr, partner).wait_send()
    remote(land.at[pl.ds(0, 31)], land.at[pl.ds(0, 31)], ms, mr, partner).wait_send()


def on_device(snapshots, space_factor):
    vm, dma = pltpu.VMEM, pltpu.SemaphoreType.DMA
    return pl.pallas_call(
        kernel,
        name="hooi_time",
        out_shape=(jax.ShapeDtypeStruct((ROWS, RANK), F32), jax.ShapeDtypeStruct((RANK // 64, COLS), F32)),
        in_specs=[pl.BlockSpec(memory_space=pl.ANY)] * 2,
        out_specs=(pl.BlockSpec(memory_space=pltpu.VMEM),) * 2,
        scratch_shapes=[
            vm((ROWS, COLS), F32), vm((COLS, RANK), F32),
            vm((ROWS, RANK), F32), vm((ROWS, RANK), F32), vm((4, ROWS // 2, RANK), F32),
            vm((NX, ROWS, RANK), F32), vm((RANK, NX * ROWS), F32),
            vm((NZ, NX, ROWS, CHUNK), F32),
            vm((NY, 8, 8, RANK + 128), F32), vm((8, 8, RANK + 128), F32), vm((NZ, 8, RANK + 128), F32),
            vm((32, 8, RANK), F32),
            vm((RANK, RANK), BF16), vm((RANK, RANK), BF16),
            vm((NZ, 2, HALF, CHUNK), F32), vm((NZ, HALF, CHUNK), F32),
            vm((4, HALF, CHUNK), F32), vm((4, HALF, CHUNK), F32),
            vm((3, HALF, CHUNK), F32), vm((3, HALF, CHUNK), F32),
            vm((2, HALF, CHUNK), F32),
            vm((32, 4, CHUNK), F32), vm((32, 4, CHUNK), F32),
            dma, dma((LOADS,)), dma, dma((NZ,)), dma((4,)), dma((4,)), dma, dma, dma, dma, dma, dma, dma, dma,
            dma((NZ,)), dma((NZ,)), dma((4,)), dma((4,)), dma((3,)), dma((3,)), dma, dma, dma, dma,
        ],
        compiler_params=pltpu.CompilerParams(collective_id=0, has_side_effects=True),
    )(snapshots, space_factor)


def solution(mesh):
    return jax.shard_map(
        on_device,
        mesh=mesh,
        in_specs=(P("tm", "space"), P("space", None)),
        out_specs=(P("tm", None), P("tm", "space")),
        check_vma=False,
    )
```

time: 757 us -> 54.5 us (0.07)
  waiting for transfers between devices: 592 us -> 0 us
  blocking collectives: 127 us -> 0 us
  Pallas kernels: 0 us -> 50.7 us
  matrix products: 15 us -> 0 us
  between operations: 15.1 us -> 0.64 us
    psum x3 -> x0, waiting for transfers between devices: 403 us -> none  [the longest x2 354 us: advance(): correlation = lax.psum(inner(current, current), 'tm')]
    unnamed x3 -> x0, waiting for transfers between devices: 190 us -> none
    psum x1 -> x0, blocking collectives: 127 us -> none  [on_device(): energy = lax.psum(jnp.sum(projected * projected), 'tm')]
    pallas_call x0 -> x1, Pallas kernels: none -> 50.7 us  [on_device(): pl.pallas_call(kernel, name='hooi_time', out_shape=(jax.ShapeDtypeStruct(...]
    dot_general x6 -> x0, matrix products: 15 us -> none  [the longest x3 7.59 us: matmul(): jnp.dot(left, right, precision=lax.Precision.HIGHEST, preferred_element_t...]
  transfers between devices with their start and end apart: 4 -> 0, of which waited for: 4 -> 0; matrix products, arithmetic and copies ran while one was open for 0% -> 0% of each run, Pallas kernels for 0% -> 0%
where the time goes in v1:
time: 54.5 us; the launch traced here: 54.3 us
  Pallas kernels  50.7 us (93%)
  local copies, waits for them, and re-layouts  2.95 us (5%)
  between operations  0.64 us (1%)
    pallas_call x1, Pallas kernels, on_device(): pl.pallas_call(kernel, name='hooi_time', out_shape=(jax.ShapeDtypeStruct(...  50.7 us
    unnamed x2, local copies, waits for them, and re-layouts  2.95 us

profile of v1, /device:TPU:1, one launch (start us, length us, event | category | flops | bytes accessed | tf_op | source)
XLA Modules:
  0.0 54.3 jit_solution(16100944422197369185)
XLA Ops:
  0.6 50.7 %hooi_time.1 = (f32[64,256]{1,0:T(8,128)}, f32[4,4096]{1,0:T(4,128)}) custom-call(f32[64,4096]{1,0:T(8,128)} %snap_hbm.1, f32[4096,256]{1,0:T(8,128)} %space_hbm.1), custom_call_target="tpu_custom_call" | custom-call | tf_op jit(solution)/shard_map/hooi_time/pallas_call | solution.py:265
  51.3 1.5 %copy.6 = f32[64,256]{1,0:T(8,128)} copy(f32[64,256]{1,0:T(8,128)} %get-tuple-element.4) | data formatting | bytes 131072
  52.8 1.5 %copy.7 = f32[4,4096]{1,0:T(4,128)} copy(f32[4,4096]{1,0:T(4,128)} %get-tuple-element.5) | data formatting | bytes 131072

commit v2 on v1

v2 whole, which is shorter than its diff:
```python
import math

import jax
import jax.numpy as jnp
from jax import lax
from jax.experimental import pallas as pl
from jax.experimental.pallas import tpu as pltpu
from jax.sharding import PartitionSpec as P

MESH = pl.DeviceIdType.MESH
F32, BF16 = jnp.float32, jnp.bfloat16
RANK = 256
TIME = 4096
NX, NY, NZ = 4, 4, 8
ROWS = 64
COLS = 4096
WIDE = COLS // NX
CHUNK = WIDE // NZ
HALF = RANK // 2
LOADS = 4
EARLY = 2
SUBS = 2
SUB = HALF // SUBS


def split(value):
    high = value.astype(BF16)
    return high, (value - high.astype(F32)).astype(BF16)


def dot(left, right, dims=((1,), (0,))):
    return lax.dot_general(left, right, (dims, ((), ())), preferred_element_type=F32)


def dot3(left, right, dims=((1,), (0,))):
    return dot(left[0], right[0], dims) + (dot(left[0], right[1], dims) + dot(left[1], right[0], dims))


def kernel(
    snap_hbm, space_hbm, time_out, load_out,
    xv, sv, py, yg, yt, xc, xg, gram, gram_x, gram_z, corr, fth, ftl, polh, poll,
    lp, lp_peer, up, up_in, down, down_in, full, mixed, land, peak_x, peak_y, peak_z,
    ld_x, ld_s, xs, xr, ys, yr, ags, agr, gxs, gxr, gzs, gzr, cs, cr, ps, pr,
    us, ur, ds, dr, fs, fr, ms, mr, pxs, pxr, pys, pyr, pzs, pzr, near,
):
    t, y = lax.axis_index("tm"), lax.axis_index("space")
    x, z, c = t // 16, (t // 2) % NZ, t % 2
    other = 1 - c

    def dev(x_, y_, z_, c_):
        return {"tm": x_ * 16 + z_ * 2 + c_, "space": y_}

    def remote(src, dst, send, recv, to):
        return pltpu.make_async_remote_copy(
            src_ref=src, dst_ref=dst, send_sem=send, recv_sem=recv, device_id=to, device_id_type=MESH
        )

    partner = dev(x, y, z, other)
    above, below = dev(x, y, (z + 1) % NZ, c), dev(x, y, (z + 7) % NZ, c)
    me8 = 2 * x + c

    def peak_of(value):
        value = jnp.max(jnp.max(value, axis=0, keepdims=True), axis=1, keepdims=True)
        return jnp.broadcast_to(value, (1, 128))

    def peak_among(ref):
        value = ref[0]
        for k in range(1, ref.shape[0]):
            value = jnp.maximum(value, ref[k])
        return value

    load_x = pltpu.make_async_copy(snap_hbm, xv, ld_x)
    load_x.start()
    depth = COLS // LOADS
    load_s = [
        pltpu.make_async_copy(space_hbm.at[pl.ds(i * depth, depth)], sv.at[pl.ds(i * depth, depth)], ld_s.at[i])
        for i in range(LOADS)
    ]
    for copy in load_s:
        copy.start()

    barrier = pltpu.get_barrier_semaphore()
    greeted = [partner, above, below] + [dev(x, (y + i) % NY, z, c) for i in (2, 1, 3)]
    greeted += [dev((x + i) % NX, y, z, k) for i in (2, 1, 3) for k in range(2)]
    for to in greeted:
        pl.semaphore_signal(barrier, inc=1, device_id=to, device_id_type=MESH)

    load_x.wait()
    acc = jnp.zeros((ROWS, RANK), F32)
    acc2 = jnp.zeros((2 * ROWS, RANK), F32)
    for i in range(LOADS):
        load_s[i].wait()
        xh, xl = split(xv[:, i * depth:(i + 1) * depth])
        sh, sl = split(sv[i * depth:(i + 1) * depth, :])
        acc2 = acc2 + dot(jnp.concatenate([xh, xl], axis=0), sh)
        acc = acc + dot(xh, sl)
    py[y] = acc2[:ROWS] + (acc2[ROWS:] + acc)
    pl.semaphore_wait(barrier, len(greeted))

    for i in (2, 1, 3):
        remote(py.at[y], py.at[y], ys, yr, dev(x, (y + i) % NY, z, c)).start()

    def pass_on(step):
        for to in (above, below):
            pl.semaphore_signal(near.at[step], inc=1, device_id=to, device_id_type=MESH)

    pass_on(0)
    peak_x[me8] = peak_of(jnp.abs(py[y]))
    for i in (2, 1, 3, 0):
        for k in range(2):
            if i or k:
                remote(peak_x.at[me8], peak_x.at[me8], pxs, pxr, dev((x + i) % NX, y, z, (c + k) % 2)).start()

    order = [(z + 4) % NZ, (z + 5) % NZ, (z + 3) % NZ, (z + 6) % NZ, (z + 2) % NZ, (z + 7) % NZ, (z + 1) % NZ, z]
    for s in range(NZ):
        for i in range(NX):
            xc[i, s] = xv[:, pl.ds(pl.multiple_of(i * WIDE + order[s] * CHUNK, CHUNK), CHUNK)]

    def send_columns(p):
        slots = pl.ds(2 * p, 2)
        for i in (2, 1, 3):
            xp = (x + i) % NX
            remote(xc.at[xp, slots], xg.at[x, slots], xs.at[p], xr.at[p], dev(xp, y, z, c)).start()

    def got_columns(p):
        some = xg.at[pl.ds(0, 3), pl.ds(2 * p, 2)]
        return remote(some, some, xs.at[p], xr.at[p], partner)

    for p in range(EARLY):
        send_columns(p)
    xg[x] = xc[x]
    pl.semaphore_wait(near.at[0], 2)
    pass_on(1)
    remote(peak_x.at[pl.ds(0, 7)], peak_x.at[pl.ds(0, 7)], pxs, pxr, partner).wait_recv()
    peak_y[y] = peak_among(peak_x)
    for i in (2, 1, 3):
        remote(peak_y.at[y], peak_y.at[y], pys, pyr, dev(x, (y + i) % NY, z, c)).start()
    pl.semaphore_wait(near.at[1], 2)
    pass_on(2)
    remote(py.at[pl.ds(0, 3)], py.at[pl.ds(0, 3)], ys, yr, partner).wait_recv()
    mine = (py[0] + py[1]) + (py[2] + py[3])

    yg[x] = mine
    for i in (2, 1, 3):
        remote(yg.at[x], yg.at[x], ags, agr, dev((x + i) % NX, y, z, c)).start()

    high, low_part = split(mine)
    share = dot(
        jnp.concatenate([high, high, low_part], axis=0), jnp.concatenate([high, low_part, high], axis=0), ((0,), (0,))
    )
    for b in range(NY):
        for k in range(8):
            gram[b, k] = share[64 * b + 8 * k:64 * b + 8 * k + 8]
    gram_x[me8] = gram[y, me8]
    for i in (2, 1, 3, 0):
        for k in range(2):
            if i or k:
                xp, cp = (x + i) % NX, (c + k) % 2
                remote(gram.at[y, 2 * xp + cp], gram_x.at[me8], gxs, gxr, dev(xp, y, z, cp)).start()
    for p in range(EARLY, NZ // 2):
        send_columns(p)

    remote(peak_y.at[pl.ds(0, 3)], peak_y.at[pl.ds(0, 3)], pys, pyr, partner).wait_recv()
    peak_z[z] = peak_among(peak_y)
    pl.semaphore_wait(near.at[2], 2)
    for i in (4, 3, 5, 2, 6, 1, 7):
        remote(peak_z.at[z], peak_z.at[z], pzs, pzr, dev(x, y, (z + i) % NZ, c)).start()

    remote(yg.at[pl.ds(0, 3)], yg.at[pl.ds(0, 3)], ags, agr, partner).wait_recv()
    for i in range(NX):
        yt[:, i * ROWS:(i + 1) * ROWS] = yg[i].T
    remote(peak_z.at[pl.ds(0, 7)], peak_z.at[pl.ds(0, 7)], pzs, pzr, partner).wait_recv()
    peak = peak_among(peak_z)[:, :1] * 1024.0

    fth[...], ftl[...] = split(yt[...] * (1.0 / peak))
    swaps = [None] * NZ

    def form(p):
        slots = (2 * p, 2 * p + 1)
        got_columns(p).wait_recv()
        cols = split(jnp.concatenate([xg[:, s].reshape(NX * ROWS, CHUNK) for s in slots], axis=1))
        value = dot3((fth[...], ftl[...]), cols)
        for i, s in enumerate(slots):
            for h in range(2):
                lp[s, h] = value[h * HALF:(h + 1) * HALF, i * CHUNK:(i + 1) * CHUNK]
            swaps[s] = remote(lp.at[s, other], lp_peer.at[s], ps.at[s], pr.at[s], partner)
            swaps[s].start()

    def held(s):
        swaps[s].wait_recv()
        return (lp[s, c] + lp_peer[s]).reshape(SUBS, SUB, CHUNK)

    ups = [[remote(up.at[s, q], up_in.at[s, q], us.at[s, q], ur.at[s, q], above) for q in range(SUBS)] for s in range(4)]
    downs = [
        [remote(down.at[s, q], down_in.at[s, q], ds.at[s, q], dr.at[s, q], below) for q in range(SUBS)] for s in range(3)
    ]

    def hop(s):
        ahead = held(2 * s)
        back = held(2 * s + 1) if s < 3 else None
        for q in range(SUBS):
            value = ahead[q]
            if s:
                ups[s - 1][q].wait_recv()
                value = value + up_in[s - 1, q]
            up[s, q] = value
            ups[s][q].start()
            if s == 3:
                continue
            value = back[q]
            if s:
                downs[s - 1][q].wait_recv()
                value = value + down_in[s - 1, q]
            down[s, q] = value
            downs[s][q].start()

    form(0)
    form(1)
    hop(0)

    remote(gram_x.at[pl.ds(0, 7)], gram_x.at[pl.ds(0, 7)], gxs, gxr, partner).wait_recv()
    total = gram_x[0]
    for k in range(1, 8):
        total = total + gram_x[k]
    gram_z[z] = total
    for i in (4, 3, 5, 2, 6, 1, 7):
        remote(gram_z.at[z], gram_z.at[z], gzs, gzr, dev(x, y, (z + i) % NZ, c)).start()

    form(2)
    hop(1)

    remote(gram_z.at[pl.ds(0, 7)], gram_z.at[pl.ds(0, 7)], gzs, gzr, partner).wait_recv()
    total = gram_z[0]
    for k in range(1, NZ):
        total = total + gram_z[k]
    block = 8 * y + me8
    corr[block] = total
    for i in (2, 1, 3, 0):
        for j in (2, 1, 3, 0):
            for k in range(2):
                if i or j or k:
                    to = dev((x + i) % NX, (y + j) % NY, z, (c + k) % 2)
                    remote(corr.at[block], corr.at[block], cs, cr, to).start()

    form(3)
    hop(2)
    hop(3)

    remote(corr.at[pl.ds(0, 31)], corr.at[pl.ds(0, 31)], cs, cr, partner).wait_recv()
    row = lax.broadcasted_iota(jnp.int32, (RANK, RANK), 0)
    col = lax.broadcasted_iota(jnp.int32, (RANK, RANK), 1)
    whole = corr[...].reshape(RANK, RANK)
    energy = jnp.sum(jnp.sum(jnp.where(row == col, whole, 0.0), axis=0, keepdims=True), axis=1, keepdims=True)
    scale = 1.0 / jnp.sqrt(energy)
    a1 = whole * scale * scale
    a1s = split(a1)
    a2 = dot3(a1s, a1s)
    a4 = dot3(split(a2), split(a2 - 9.0 * a1))
    poly = jnp.where(row == col, 2.25, 0.0) + (a4 + (27.0 * a2 - 39.0 * a1)) * 0.0625
    high, low_part = split(poly)
    for h in range(2):
        polh[h] = high[:, h * HALF:(h + 1) * HALF]
        poll[h] = low_part[:, h * HALF:(h + 1) * HALF]

    last = held(NZ - 1)
    for q in range(SUBS):
        downs[2][q].wait_recv()
        ups[3][q].wait_recv()
        full[c, q * SUB:(q + 1) * SUB] = (last[q] + down_in[2, q] + up_in[3, q]) * (peak * scale)
    share_full = remote(full.at[c], full.at[c], fs, fr, partner)
    share_full.start()
    value = dot3((polh[c], poll[c]), split(full[c]))
    share_full.wait_recv()
    value = value + dot3((polh[other], poll[other]), split(full[other]))
    value = jnp.where(c == 0, value, pltpu.roll(value, RANK - 4, 0))
    for k in range(NX * NZ):
        mixed[k] = value[8 * k:8 * k + 4]
    spot = NZ * x + z
    land[spot] = mixed[spot]
    for i in (2, 1, 3, 0):
        for j in (4, 3, 5, 2, 6, 1, 7, 0):
            if i or j:
                xp, zp = (x + i) % NX, (z + j) % NZ
                remote(mixed.at[NZ * xp + zp], land.at[spot], ms, mr, dev(xp, y, zp, c)).start()
    time_out[...] = dot3(split(yg[x] * scale), (high, low_part)) * math.sqrt(TIME)
    remote(land.at[pl.ds(0, 31)], land.at[pl.ds(0, 31)], ms, mr, partner).wait_recv()
    for k in range(NX * NZ):
        load_out[:, k * CHUNK:(k + 1) * CHUNK] = land[k]

    for copy in swaps + sum(ups + downs, []) + [share_full] + [got_columns(p) for p in range(NZ // 2)]:
        copy.wait_send()
    remote(py.at[pl.ds(0, 3)], py.at[pl.ds(0, 3)], ys, yr, partner).wait_send()
    remote(yg.at[pl.ds(0, 3)], yg.at[pl.ds(0, 3)], ags, agr, partner).wait_send()
    remote(gram_x.at[pl.ds(0, 7)], gram_x.at[pl.ds(0, 7)], gxs, gxr, partner).wait_send()
    remote(gram_z.at[pl.ds(0, 7)], gram_z.at[pl.ds(0, 7)], gzs, gzr, partner).wait_send()
    remote(corr.at[pl.ds(0, 31)], corr.at[pl.ds(0, 31)], cs, cr, partner).wait_send()
    remote(land.at[pl.ds(0, 31)], land.at[pl.ds(0, 31)], ms, mr, partner).wait_send()
    remote(peak_x.at[pl.ds(0, 7)], peak_x.at[pl.ds(0, 7)], pxs, pxr, partner).wait_send()
    remote(peak_y.at[pl.ds(0, 3)], peak_y.at[pl.ds(0, 3)], pys, pyr, partner).wait_send()
    remote(peak_z.at[pl.ds(0, 7)], peak_z.at[pl.ds(0, 7)], pzs, pzr, partner).wait_send()


def on_device(snapshots, space_factor):
    vm, dma = pltpu.VMEM, pltpu.SemaphoreType.DMA
    return pl.pallas_call(
        kernel,
        name="hooi_time",
        out_shape=(jax.ShapeDtypeStruct((ROWS, RANK), F32), jax.ShapeDtypeStruct((RANK // 64, COLS), F32)),
        in_specs=[pl.BlockSpec(memory_space=pl.ANY)] * 2,
        out_specs=(pl.BlockSpec(memory_space=pltpu.VMEM),) * 2,
        scratch_shapes=[
            vm((ROWS, COLS), F32), vm((COLS, RANK), F32), vm((NY, ROWS, RANK), F32),
            vm((NX, ROWS, RANK), F32), vm((RANK, NX * ROWS), F32),
            vm((NX, NZ, ROWS, CHUNK), F32), vm((NX, NZ, ROWS, CHUNK), F32),
            vm((NY, 8, 8, RANK), F32), vm((8, 8, RANK), F32), vm((NZ, 8, RANK), F32),
            vm((32, 8, RANK), F32),
            vm((RANK, RANK), BF16), vm((RANK, RANK), BF16),
            vm((2, RANK, HALF), BF16), vm((2, RANK, HALF), BF16),
            vm((NZ, 2, HALF, CHUNK), F32), vm((NZ, HALF, CHUNK), F32),
            vm((4, SUBS, SUB, CHUNK), F32), vm((4, SUBS, SUB, CHUNK), F32),
            vm((3, SUBS, SUB, CHUNK), F32), vm((3, SUBS, SUB, CHUNK), F32),
            vm((2, HALF, CHUNK), F32),
            vm((32, 4, CHUNK), F32), vm((32, 4, CHUNK), F32),
            vm((8, 1, 128), F32), vm((NY, 1, 128), F32), vm((NZ, 1, 128), F32),
            dma, dma((LOADS,)), dma((4,)), dma((4,)), dma, dma, dma, dma, dma, dma, dma, dma, dma, dma,
            dma((NZ,)), dma((NZ,)), dma((4, SUBS)), dma((4, SUBS)), dma((3, SUBS)), dma((3, SUBS)), dma, dma, dma, dma,
            dma, dma, dma, dma, dma, dma, pltpu.SemaphoreType.REGULAR((3,)),
        ],
        compiler_params=pltpu.CompilerParams(collective_id=0, has_side_effects=True),
    )(snapshots, space_factor)


def solution(mesh):
    return jax.shard_map(
        on_device,
        mesh=mesh,
        in_specs=(P("tm", "space"), P("space", None)),
        out_specs=(P("tm", None), P("tm", "space")),
        check_vma=False,
    )
```

time: 54.5 us -> 49.1 us (0.901)
  Pallas kernels: 50.7 us -> 45.3 us
    pallas_call x1, Pallas kernels: 50.7 us -> 45.3 us  [on_device(): pl.pallas_call(kernel, name='hooi_time', out_shape=(jax.ShapeDtypeStruct(...]
where the time goes in v2:
time: 49.1 us; the launch traced here: 48.9 us
  Pallas kernels  45.3 us (92%)
  local copies, waits for them, and re-layouts  2.95 us (6%)
  between operations  0.64 us (1%)
    pallas_call x1, Pallas kernels, on_device(): pl.pallas_call(kernel, name='hooi_time', out_shape=(jax.ShapeDtypeStruct(...  45.3 us
    unnamed x2, local copies, waits for them, and re-layouts  2.95 us

profile of v2, /device:TPU:1, one launch (start us, length us, event | category | flops | bytes accessed | tf_op | source)
XLA Modules:
  0.0 48.9 jit_solution(1132860009648391444)
XLA Ops:
  0.6 45.3 %hooi_time.1 = (f32[64,256]{1,0:T(8,128)}, f32[4,4096]{1,0:T(4,128)}) custom-call(f32[64,4096]{1,0:T(8,128)} %snap_hbm.1, f32[4096,256]{1,0:T(8,128)} %space_hbm.1), custom_call_target="tpu_custom_call" | custom-call | tf_op jit(solution)/shard_map/hooi_time/pallas_call | solution.py:305
  46.0 1.5 %copy.6 = f32[64,256]{1,0:T(8,128)} copy(f32[64,256]{1,0:T(8,128)} %get-tuple-element.4) | data formatting | bytes 131072
  47.4 1.5 %copy.7 = f32[4,4096]{1,0:T(4,128)} copy(f32[4,4096]{1,0:T(4,128)} %get-tuple-element.5) | data formatting | bytes 131072

commit v3 on v2

--- a/solution.py
+++ b/solution.py
@@ -144,27 +144,28 @@
     for i in (2, 1, 3):
         remote(yg.at[x], yg.at[x], ags, agr, dev((x + i) % NX, y, z, c)).start()
 
-    high, low_part = split(mine)
-    share = dot(
-        jnp.concatenate([high, high, low_part], axis=0), jnp.concatenate([high, low_part, high], axis=0), ((0,), (0,))
-    )
-    for b in range(NY):
-        for k in range(8):
-            gram[b, k] = share[64 * b + 8 * k:64 * b + 8 * k + 8]
-    gram_x[me8] = gram[y, me8]
-    for i in (2, 1, 3, 0):
-        for k in range(2):
-            if i or k:
-                xp, cp = (x + i) % NX, (c + k) % 2
-                remote(gram.at[y, 2 * xp + cp], gram_x.at[me8], gxs, gxr, dev(xp, y, z, cp)).start()
-    for p in range(EARLY, NZ // 2):
-        send_columns(p)
-
     remote(peak_y.at[pl.ds(0, 3)], peak_y.at[pl.ds(0, 3)], pys, pyr, partner).wait_recv()
     peak_z[z] = peak_among(peak_y)
     pl.semaphore_wait(near.at[2], 2)
     for i in (4, 3, 5, 2, 6, 1, 7):
         remote(peak_z.at[z], peak_z.at[z], pzs, pzr, dev(x, y, (z + i) % NZ, c)).start()
+
+    left = split(yg[x, :, pl.ds(pl.multiple_of(y // 2 * HALF, HALF), HALF)])
+    high, low_part = split(mine)
+    share = dot(
+        jnp.concatenate([left[0], left[0], left[1]], axis=0), jnp.concatenate([high, low_part, high], axis=0), ((0,), (0,))
+    )
+    for b in range(2):
+        for k in range(8):
+            gram[b, k] = share[64 * b + 8 * k:64 * b + 8 * k + 8]
+    gram_x[me8] = gram[y % 2, me8]
+    for i in (2, 1, 3, 0):
+        for k in range(2):
+            if i or k:
+                xp, cp = (x + i) % NX, (c + k) % 2
+                remote(gram.at[y % 2, 2 * xp + cp], gram_x.at[me8], gxs, gxr, dev(xp, y, z, cp)).start()
+    for p in range(EARLY, NZ // 2):
+        send_columns(p)
 
     remote(yg.at[pl.ds(0, 3)], yg.at[pl.ds(0, 3)], ags, agr, partner).wait_recv()
     for i in range(NX):
@@ -300,19 +301,27 @@
     remote(peak_z.at[pl.ds(0, 7)], peak_z.at[pl.ds(0, 7)], pzs, pzr, partner).wait_send()
 
 
+def put_out(time, load, time_hbm, load_hbm, time_sem, load_sem):
+    copies = [pltpu.make_async_copy(time, time_hbm, time_sem), pltpu.make_async_copy(load, load_hbm, load_sem)]
+    for copy in copies:
+        copy.start()
+    for copy in copies:
+        copy.wait()
+
+
 def on_device(snapshots, space_factor):
     vm, dma = pltpu.VMEM, pltpu.SemaphoreType.DMA
-    return pl.pallas_call(
+    time, load = pl.pallas_call(
         kernel,
         name="hooi_time",
-        out_shape=(jax.ShapeDtypeStruct((ROWS, RANK), F32), jax.ShapeDtypeStruct((RANK // 64, COLS), F32)),
+        out_shape=(vm((ROWS, RANK), F32), vm((RANK // 64, COLS), F32)),
         in_specs=[pl.BlockSpec(memory_space=pl.ANY)] * 2,
         out_specs=(pl.BlockSpec(memory_space=pltpu.VMEM),) * 2,
         scratch_shapes=[
             vm((ROWS, COLS), F32), vm((COLS, RANK), F32), vm((NY, ROWS, RANK), F32),
             vm((NX, ROWS, RANK), F32), vm((RANK, NX * ROWS), F32),
             vm((NX, NZ, ROWS, CHUNK), F32), vm((NX, NZ, ROWS, CHUNK), F32),
-            vm((NY, 8, 8, RANK), F32), vm((8, 8, RANK), F32), vm((NZ, 8, RANK), F32),
+            vm((2, 8, 8, RANK), F32), vm((8, 8, RANK), F32), vm((NZ, 8, RANK), F32),
             vm((32, 8, RANK), F32),
             vm((RANK, RANK), BF16), vm((RANK, RANK), BF16),
             vm((2, RANK, HALF), BF16), vm((2, RANK, HALF), BF16),
@@ -328,6 +337,14 @@
         ],
         compiler_params=pltpu.CompilerParams(collective_id=0, has_side_effects=True),
     )(snapshots, space_factor)
+    return pl.pallas_call(
+        put_out,
+        name="put_out",
+        out_shape=(jax.ShapeDtypeStruct(time.shape, F32), jax.ShapeDtypeStruct(load.shape, F32)),
+        in_specs=[pl.BlockSpec(memory_space=pltpu.VMEM)] * 2,
+        out_specs=(pl.BlockSpec(memory_space=pl.ANY),) * 2,
+        scratch_shapes=[dma, dma],
+    )(pltpu.with_memory_space_constraint(time, pltpu.VMEM), pltpu.with_memory_space_constraint(load, pltpu.VMEM))
 
 
 def solution(mesh):

time: 49.1 us -> 46 us (0.937)
  local copies, waits for them, and re-layouts: 2.95 us -> 0 us
    unnamed x2 -> x0, local copies, waits for them, and re-layouts: 2.95 us -> none
    pallas_call x1 -> x2, Pallas kernels: 45.3 us -> 45.3 us  [the longest x1 44.6 us: on_device(): pl.pallas_call(kernel, name='hooi_time', out_shape=(vm((ROWS, RANK), F32)...]
where the time goes in v3:
time: 46 us; the launch traced here: 45.9 us
  Pallas kernels  45.3 us (98%)
  between operations  0.64 us (1%)
    pallas_call x1, Pallas kernels, on_device(): pl.pallas_call(kernel, name='hooi_time', out_shape=(vm((ROWS, RANK), F32)...  44.6 us

profile of v3, /device:TPU:1, one launch (start us, length us, event | category | flops | bytes accessed | tf_op | source)
XLA Modules:
  0.0 45.9 jit_solution(5722085791025986352)
XLA Ops:
  0.6 44.6 %hooi_time.1 = (f32[64,256]{1,0:T(8,128)S(1)}, f32[4,4096]{1,0:T(4,128)S(1)}) custom-call(f32[64,4096]{1,0:T(8,128)} %snap_hbm.1, f32[4096,256]{1,0:T(8,128)} %space_hbm.1), custom_call_target="tpu_custom_call" | custom-call | tf_op jit(solution)/shard_map/hooi_time/pallas_call | solution.py:314
  45.2 0.7 %put_out.1 = (f32[64,256]{1,0:T(8,128)}, f32[4,4096]{1,0:T(4,128)}) custom-call(f32[64,256]{1,0:T(8,128)S(1)} %get-tuple-element.4.time, f32[4,4096]{1,0:T(4,128)S(1)} %get-tuple-element.5.load), custom_call_target="tpu_custom_call" | custom-call | tf_op jit(solution)/shard_map/put_out/pallas_call | solution.py:340

commit v4 on v3

--- a/solution.py
+++ b/solution.py
@@ -17,7 +17,7 @@
 WIDE = COLS // NX
 CHUNK = WIDE // NZ
 HALF = RANK // 2
-LOADS = 4
+LOADS = 8
 EARLY = 2
 SUBS = 2
 SUB = HALF // SUBS
@@ -39,7 +39,7 @@
 def kernel(
     snap_hbm, space_hbm, time_out, load_out,
     xv, sv, py, yg, yt, xc, xg, gram, gram_x, gram_z, corr, fth, ftl, polh, poll,
-    lp, lp_peer, up, up_in, down, down_in, full, mixed, land, peak_x, peak_y, peak_z,
+    lp, lp_peer, up, up_in, down, down_in, full, mixed, peak_x, peak_y, peak_z,
     ld_x, ld_s, xs, xr, ys, yr, ags, agr, gxs, gxr, gzs, gzr, cs, cr, ps, pr,
     us, ur, ds, dr, fs, fr, ms, mr, pxs, pxr, pys, pyr, pzs, pzr, near,
 ):
@@ -69,14 +69,13 @@
             value = jnp.maximum(value, ref[k])
         return value
 
-    load_x = pltpu.make_async_copy(snap_hbm, xv, ld_x)
-    load_x.start()
     depth = COLS // LOADS
-    load_s = [
-        pltpu.make_async_copy(space_hbm.at[pl.ds(i * depth, depth)], sv.at[pl.ds(i * depth, depth)], ld_s.at[i])
-        for i in range(LOADS)
-    ]
-    for copy in load_s:
+    loads = []
+    for i in range(LOADS):
+        piece = pl.ds(i * depth, depth)
+        loads.append(pltpu.make_async_copy(snap_hbm.at[:, piece], xv.at[:, piece], ld_x.at[i]))
+        loads.append(pltpu.make_async_copy(space_hbm.at[piece], sv.at[piece], ld_s.at[i]))
+    for copy in loads:
         copy.start()
 
     barrier = pltpu.get_barrier_semaphore()
@@ -85,11 +84,11 @@
     for to in greeted:
         pl.semaphore_signal(barrier, inc=1, device_id=to, device_id_type=MESH)
 
-    load_x.wait()
     acc = jnp.zeros((ROWS, RANK), F32)
     acc2 = jnp.zeros((2 * ROWS, RANK), F32)
     for i in range(LOADS):
-        load_s[i].wait()
+        loads[2 * i].wait()
+        loads[2 * i + 1].wait()
         xh, xl = split(xv[:, i * depth:(i + 1) * depth])
         sh, sl = split(sv[i * depth:(i + 1) * depth, :])
         acc2 = acc2 + dot(jnp.concatenate([xh, xl], axis=0), sh)
@@ -141,14 +140,6 @@
     mine = (py[0] + py[1]) + (py[2] + py[3])
 
     yg[x] = mine
-    for i in (2, 1, 3):
-        remote(yg.at[x], yg.at[x], ags, agr, dev((x + i) % NX, y, z, c)).start()
-
-    remote(peak_y.at[pl.ds(0, 3)], peak_y.at[pl.ds(0, 3)], pys, pyr, partner).wait_recv()
-    peak_z[z] = peak_among(peak_y)
-    pl.semaphore_wait(near.at[2], 2)
-    for i in (4, 3, 5, 2, 6, 1, 7):
-        remote(peak_z.at[z], peak_z.at[z], pzs, pzr, dev(x, y, (z + i) % NZ, c)).start()
 
     left = split(yg[x, :, pl.ds(pl.multiple_of(y // 2 * HALF, HALF), HALF)])
     high, low_part = split(mine)
@@ -164,6 +155,15 @@
             if i or k:
                 xp, cp = (x + i) % NX, (c + k) % 2
                 remote(gram.at[y % 2, 2 * xp + cp], gram_x.at[me8], gxs, gxr, dev(xp, y, z, cp)).start()
+    for i in (2, 1, 3):
+        remote(yg.at[x], yg.at[x], ags, agr, dev((x + i) % NX, y, z, c)).start()
+
+    remote(peak_y.at[pl.ds(0, 3)], peak_y.at[pl.ds(0, 3)], pys, pyr, partner).wait_recv()
+    peak_z[z] = peak_among(peak_y)
+    pl.semaphore_wait(near.at[2], 2)
+    for i in (4, 3, 5, 2, 6, 1, 7):
+        remote(peak_z.at[z], peak_z.at[z], pzs, pzr, dev(x, y, (z + i) % NZ, c)).start()
+
     for p in range(EARLY, NZ // 2):
         send_columns(p)
 
@@ -191,33 +191,36 @@
         swaps[s].wait_recv()
         return (lp[s, c] + lp_peer[s]).reshape(SUBS, SUB, CHUNK)
 
-    ups = [[remote(up.at[s, q], up_in.at[s, q], us.at[s, q], ur.at[s, q], above) for q in range(SUBS)] for s in range(4)]
+    up_to = [above, dev(x, y, (z + 2) % NZ, c), above, above]
+    ups = [
+        [remote(up.at[s, q], up_in.at[s, q], us.at[s, q], ur.at[s, q], up_to[s]) for q in range(SUBS)] for s in range(4)
+    ]
     downs = [
         [remote(down.at[s, q], down_in.at[s, q], ds.at[s, q], dr.at[s, q], below) for q in range(SUBS)] for s in range(3)
     ]
 
-    def hop(s):
-        ahead = held(2 * s)
-        back = held(2 * s + 1) if s < 3 else None
+    def send_up(s, slot, joins):
+        block = held(slot)
         for q in range(SUBS):
-            value = ahead[q]
-            if s:
-                ups[s - 1][q].wait_recv()
-                value = value + up_in[s - 1, q]
+            value = block[q]
+            for k in joins:
+                ups[k][q].wait_recv()
+                value = value + up_in[k, q]
             up[s, q] = value
             ups[s][q].start()
-            if s == 3:
-                continue
-            value = back[q]
-            if s:
-                downs[s - 1][q].wait_recv()
-                value = value + down_in[s - 1, q]
+
+    def send_down(s, slot, joins):
+        block = held(slot)
+        for q in range(SUBS):
+            value = block[q]
+            for k in joins:
+                downs[k][q].wait_recv()
+                value = value + down_in[k, q]
             down[s, q] = value
             downs[s][q].start()
 
     form(0)
     form(1)
-    hop(0)
 
     remote(gram_x.at[pl.ds(0, 7)], gram_x.at[pl.ds(0, 7)], gxs, gxr, partner).wait_recv()
     total = gram_x[0]
@@ -227,8 +230,11 @@
     for i in (4, 3, 5, 2, 6, 1, 7):
         remote(gram_z.at[z], gram_z.at[z], gzs, gzr, dev(x, y, (z + i) % NZ, c)).start()
 
+    send_up(0, 0, ())
+    send_down(0, 1, ())
+
     form(2)
-    hop(1)
+    send_up(1, 2, (0,))
 
     remote(gram_z.at[pl.ds(0, 7)], gram_z.at[pl.ds(0, 7)], gzs, gzr, partner).wait_recv()
     total = gram_z[0]
@@ -243,9 +249,12 @@
                     to = dev((x + i) % NX, (y + j) % NY, z, (c + k) % 2)
                     remote(corr.at[block], corr.at[block], cs, cr, to).start()
 
+    send_down(1, 3, (0,))
+    send_up(2, 4, ())
+
     form(3)
-    hop(2)
-    hop(3)
+    send_down(2, 5, (1,))
+    send_up(3, 6, (2, 1))
 
     remote(corr.at[pl.ds(0, 31)], corr.at[pl.ds(0, 31)], cs, cr, partner).wait_recv()
     row = lax.broadcasted_iota(jnp.int32, (RANK, RANK), 0)
@@ -277,16 +286,15 @@
     for k in range(NX * NZ):
         mixed[k] = value[8 * k:8 * k + 4]
     spot = NZ * x + z
-    land[spot] = mixed[spot]
+    here = pl.ds(pl.multiple_of(spot * CHUNK, CHUNK), CHUNK)
+    load_out[:, here] = mixed[spot]
     for i in (2, 1, 3, 0):
         for j in (4, 3, 5, 2, 6, 1, 7, 0):
             if i or j:
                 xp, zp = (x + i) % NX, (z + j) % NZ
-                remote(mixed.at[NZ * xp + zp], land.at[spot], ms, mr, dev(xp, y, zp, c)).start()
+                remote(mixed.at[NZ * xp + zp], load_out.at[:, here], ms, mr, dev(xp, y, zp, c)).start()
     time_out[...] = dot3(split(yg[x] * scale), (high, low_part)) * math.sqrt(TIME)
-    remote(land.at[pl.ds(0, 31)], land.at[pl.ds(0, 31)], ms, mr, partner).wait_recv()
-    for k in range(NX * NZ):
-        load_out[:, k * CHUNK:(k + 1) * CHUNK] = land[k]
+    remote(mixed.at[pl.ds(0, 31)], mixed.at[pl.ds(0, 31)], ms, mr, partner).wait_recv()
 
     for copy in swaps + sum(ups + downs, []) + [share_full] + [got_columns(p) for p in range(NZ // 2)]:
         copy.wait_send()
@@ -295,7 +303,7 @@
     remote(gram_x.at[pl.ds(0, 7)], gram_x.at[pl.ds(0, 7)], gxs, gxr, partner).wait_send()
     remote(gram_z.at[pl.ds(0, 7)], gram_z.at[pl.ds(0, 7)], gzs, gzr, partner).wait_send()
     remote(corr.at[pl.ds(0, 31)], corr.at[pl.ds(0, 31)], cs, cr, partner).wait_send()
-    remote(land.at[pl.ds(0, 31)], land.at[pl.ds(0, 31)], ms, mr, partner).wait_send()
+    remote(mixed.at[pl.ds(0, 31)], mixed.at[pl.ds(0, 31)], ms, mr, partner).wait_send()
     remote(peak_x.at[pl.ds(0, 7)], peak_x.at[pl.ds(0, 7)], pxs, pxr, partner).wait_send()
     remote(peak_y.at[pl.ds(0, 3)], peak_y.at[pl.ds(0, 3)], pys, pyr, partner).wait_send()
     remote(peak_z.at[pl.ds(0, 7)], peak_z.at[pl.ds(0, 7)], pzs, pzr, partner).wait_send()
@@ -329,9 +337,9 @@
             vm((4, SUBS, SUB, CHUNK), F32), vm((4, SUBS, SUB, CHUNK), F32),
             vm((3, SUBS, SUB, CHUNK), F32), vm((3, SUBS, SUB, CHUNK), F32),
             vm((2, HALF, CHUNK), F32),
-            vm((32, 4, CHUNK), F32), vm((32, 4, CHUNK), F32),
+            vm((32, 4, CHUNK), F32),
             vm((8, 1, 128), F32), vm((NY, 1, 128), F32), vm((NZ, 1, 128), F32),
-            dma, dma((LOADS,)), dma((4,)), dma((4,)), dma, dma, dma, dma, dma, dma, dma, dma, dma, dma,
+            dma((LOADS,)), dma((LOADS,)), dma((4,)), dma((4,)), dma, dma, dma, dma, dma, dma, dma, dma, dma, dma,
             dma((NZ,)), dma((NZ,)), dma((4, SUBS)), dma((4, SUBS)), dma((3, SUBS)), dma((3, SUBS)), dma, dma, dma, dma,
             dma, dma, dma, dma, dma, dma, pltpu.SemaphoreType.REGULAR((3,)),
         ],

time: 46 us -> 44.9 us (0.976)
  Pallas kernels: 45.3 us -> 44.2 us
    pallas_call x1, Pallas kernels: 44.6 us -> 43.5 us  [on_device(): pl.pallas_call(kernel, name='hooi_time', out_shape=(vm((ROWS, RANK), F32)...]
where the time goes in v4:
time: 44.9 us; the launch traced here: 44.8 us
  Pallas kernels  44.2 us (98%)
  between operations  0.64 us (1%)
    pallas_call x1, Pallas kernels, on_device(): pl.pallas_call(kernel, name='hooi_time', out_shape=(vm((ROWS, RANK), F32)...  43.5 us

profile of v4, /device:TPU:1, one launch (start us, length us, event | category | flops | bytes accessed | tf_op | source)
XLA Modules:
  0.0 44.8 jit_solution(8516211684624667531)
XLA Ops:
  0.6 43.5 %hooi_time.1 = (f32[64,256]{1,0:T(8,128)S(1)}, f32[4,4096]{1,0:T(4,128)S(1)}) custom-call(f32[64,4096]{1,0:T(8,128)} %snap_hbm.1, f32[4096,256]{1,0:T(8,128)} %space_hbm.1), custom_call_target="tpu_custom_call" | custom-call | tf_op jit(solution)/shard_map/hooi_time/pallas_call | solution.py:322
  44.1 0.7 %put_out.1 = (f32[64,256]{1,0:T(8,128)}, f32[4,4096]{1,0:T(4,128)}) custom-call(f32[64,256]{1,0:T(8,128)S(1)} %get-tuple-element.4.time, f32[4,4096]{1,0:T(4,128)S(1)} %get-tuple-element.5.load), custom_call_target="tpu_custom_call" | custom-call | tf_op jit(solution)/shard_map/put_out/pallas_call | solution.py:348

commit v5 on v4

--- a/solution.py
+++ b/solution.py
@@ -19,7 +19,7 @@
 HALF = RANK // 2
 LOADS = 8
 EARLY = 2
-SUBS = 2
+SUBS = 4
 SUB = HALF // SUBS
 
 
@@ -140,6 +140,16 @@
     mine = (py[0] + py[1]) + (py[2] + py[3])
 
     yg[x] = mine
+
+    for i in (2, 1, 3):
+        remote(yg.at[x], yg.at[x], ags, agr, dev((x + i) % NX, y, z, c)).start()
+
+    remote(peak_y.at[pl.ds(0, 3)], peak_y.at[pl.ds(0, 3)], pys, pyr, partner).wait_recv()
+    peak_z[z] = peak_among(peak_y)
+    pl.semaphore_wait(near.at[2], 2)
+    for i in (4, 3, 5, 2, 6, 1, 7):
+        remote(peak_z.at[z], peak_z.at[z], pzs, pzr, dev(x, y, (z + i) % NZ, c)).start()
+
 
     left = split(yg[x, :, pl.ds(pl.multiple_of(y // 2 * HALF, HALF), HALF)])
     high, low_part = split(mine)
@@ -155,15 +165,6 @@
             if i or k:
                 xp, cp = (x + i) % NX, (c + k) % 2
                 remote(gram.at[y % 2, 2 * xp + cp], gram_x.at[me8], gxs, gxr, dev(xp, y, z, cp)).start()
-    for i in (2, 1, 3):
-        remote(yg.at[x], yg.at[x], ags, agr, dev((x + i) % NX, y, z, c)).start()
-
-    remote(peak_y.at[pl.ds(0, 3)], peak_y.at[pl.ds(0, 3)], pys, pyr, partner).wait_recv()
-    peak_z[z] = peak_among(peak_y)
-    pl.semaphore_wait(near.at[2], 2)
-    for i in (4, 3, 5, 2, 6, 1, 7):
-        remote(peak_z.at[z], peak_z.at[z], pzs, pzr, dev(x, y, (z + i) % NZ, c)).start()
-
     for p in range(EARLY, NZ // 2):
         send_columns(p)
 

time: 44.9 us -> 44.6 us (level)
  no operation moved by 1% of the time
where the time goes in v5:
time: 44.6 us; the launch traced here: 44.5 us
  Pallas kernels  43.8 us (98%)
  between operations  0.64 us (1%)
    pallas_call x1, Pallas kernels, on_device(): pl.pallas_call(kernel, name='hooi_time', out_shape=(vm((ROWS, RANK), F32)...  43.2 us

profile of v5, /device:TPU:1, one launch (start us, length us, event | category | flops | bytes accessed | tf_op | source)
XLA Modules:
  0.0 44.5 jit_solution(2034623418900524100)
XLA Ops:
  0.6 43.2 %hooi_time.1 = (f32[64,256]{1,0:T(8,128)S(1)}, f32[4,4096]{1,0:T(4,128)S(1)}) custom-call(f32[64,4096]{1,0:T(8,128)} %snap_hbm.1, f32[4096,256]{1,0:T(8,128)} %space_hbm.1), custom_call_target="tpu_custom_call" | custom-call | tf_op jit(solution)/shard_map/hooi_time/pallas_call | solution.py:323
  43.8 0.7 %put_out.1 = (f32[64,256]{1,0:T(8,128)}, f32[4,4096]{1,0:T(4,128)}) custom-call(f32[64,256]{1,0:T(8,128)S(1)} %get-tuple-element.4.time, f32[4,4096]{1,0:T(4,128)S(1)} %get-tuple-element.5.load), custom_call_target="tpu_custom_call" | custom-call | tf_op jit(solution)/shard_map/put_out/pallas_call | solution.py:349

commit v6 on v5

--- a/solution.py
+++ b/solution.py
@@ -165,8 +165,7 @@
             if i or k:
                 xp, cp = (x + i) % NX, (c + k) % 2
                 remote(gram.at[y % 2, 2 * xp + cp], gram_x.at[me8], gxs, gxr, dev(xp, y, z, cp)).start()
-    for p in range(EARLY, NZ // 2):
-        send_columns(p)
+    send_columns(2)
 
     remote(yg.at[pl.ds(0, 3)], yg.at[pl.ds(0, 3)], ags, agr, partner).wait_recv()
     for i in range(NX):
@@ -231,6 +230,7 @@
     for i in (4, 3, 5, 2, 6, 1, 7):
         remote(gram_z.at[z], gram_z.at[z], gzs, gzr, dev(x, y, (z + i) % NZ, c)).start()
 
+    send_columns(3)
     send_up(0, 0, ())
     send_down(0, 1, ())
 

time: 44.6 us -> 44.6 us (level)
  no operation moved by 1% of the time
where the time goes in v6:
time: 44.6 us; the launch traced here: 44.5 us
  Pallas kernels  43.8 us (98%)
  between operations  0.64 us (1%)
    pallas_call x1, Pallas kernels, on_device(): pl.pallas_call(kernel, name='hooi_time', out_shape=(vm((ROWS, RANK), F32)...  43.2 us

profile of v6, /device:TPU:1, one launch (start us, length us, event | category | flops | bytes accessed | tf_op | source)
XLA Modules:
  0.0 44.5 jit_solution(15837694468667460024)
XLA Ops:
  0.6 43.2 %hooi_time.1 = (f32[64,256]{1,0:T(8,128)S(1)}, f32[4,4096]{1,0:T(4,128)S(1)}) custom-call(f32[64,4096]{1,0:T(8,128)} %snap_hbm.1, f32[4096,256]{1,0:T(8,128)} %space_hbm.1), custom_call_target="tpu_custom_call" | custom-call | tf_op jit(solution)/shard_map/hooi_time/pallas_call | solution.py:323
  43.8 0.7 %put_out.1 = (f32[64,256]{1,0:T(8,128)}, f32[4,4096]{1,0:T(4,128)}) custom-call(f32[64,256]{1,0:T(8,128)S(1)} %get-tuple-element.4.time, f32[4,4096]{1,0:T(4,128)S(1)} %get-tuple-element.5.load), custom_call_target="tpu_custom_call" | custom-call | tf_op jit(solution)/shard_map/put_out/pallas_call | solution.py:349
